TPU v7x, 512 devices: a whole 4x8x8 slice. The times are simulated.
512 devices in a mesh: dp: 16 (over z, core), tp: 4 (over y_lo), cp: 8 (over y_hi, x).
Axes of the slice: x: 4, y: 8 (y_hi: 2, y_lo: 4; y = y_hi * 4 + y_lo), z: 8, core: 2. Of those that a mesh axis runs over, the one named last changes fastest.
Arguments:
- tokens: bfloat16 [65536, 1024], P(('dp', 'tp', 'cp')), may hold values from -6 to 6
- expert_ids: int32 [65536, 2], P(('dp', 'tp', 'cp')), may hold values from 0 to 31, all different within a row; in each aligned block of 128 rows (0 to 127, 128 to 255, ...) at most 12 rows name the same one
- router_weight: bfloat16 [1024, 32], replicated, may hold values from -0.1875 to 0.1875
- gate_weight: bfloat16 [32, 1024, 384], P(('tp', 'cp'), 'dp'), may hold values from -0.1875 to 0.1875
- up_weight: bfloat16 [32, 1024, 384], P(('tp', 'cp'), 'dp'), may hold values from -0.1875 to 0.1875
- down_weight: bfloat16 [32, 384, 1024], P(('tp', 'cp'), None, 'dp'), may hold values from -0.3125 to 0.3125
- grad_out: bfloat16 [65536, 1024], P(('dp', 'tp', 'cp')), may hold values from -6 to 6
Outputs:
- moe_out: bfloat16 [65536, 1024], P(('dp', 'tp', 'cp'))
- grad_tokens: bfloat16 [65536, 1024], P(('dp', 'tp', 'cp'))
- router_grad: float32 [1024, 32], replicated
Inputs may be any that keep to these rules, and one draw needn't show every extreme that they name: `expert_ids`: each row names 2 different experts. Among the 128 rows of one device no expert is named by more than 12 rows, a bound that some block reaches.
All inputs are finite; a program needn't handle non-finite values.
Results may differ from a plain program's by a relative error of at most 0.0064.
Values may be sent and summed in bfloat16 or wider, within the bound.
A program may use at most 64 MiB of HBM per device.

v0:
```python
import jax
import jax.numpy as jnp
from jax import lax
from jax.sharding import PartitionSpec as P


def route_slots(flat_ids, expert_count):
    hits = (flat_ids[:, None] == jnp.arange(expert_count, dtype=jnp.int32)[None, :]).astype(
        jnp.int32
    )
    before = jnp.cumsum(hits, axis=0) - hits
    return jnp.sum(before * hits, axis=1)


def trade(stacked, capacity):
    item_count = stacked.shape[0]
    feature_dim = stacked.shape[2]
    tp_count = lax.axis_size("tp")
    cp_count = lax.axis_size("cp")
    shaped = stacked.reshape(item_count, tp_count * cp_count, capacity, feature_dim)
    moved = lax.all_to_all(shaped, ("tp", "cp"), split_axis=1, concat_axis=1, tiled=True)
    return moved.reshape(item_count, -1, feature_dim)


def expert_forward(received, w_gate, w_up, w_down):
    gate_act = jnp.dot(received, w_gate, preferred_element_type=jnp.float32)
    up_act = jnp.dot(received, w_up, preferred_element_type=jnp.float32)
    hidden = (jax.nn.silu(gate_act) * up_act).astype(jnp.bfloat16)
    produced = jnp.dot(hidden, w_down, preferred_element_type=jnp.float32).astype(jnp.bfloat16)
    return (gate_act, up_act, produced)


def expert_backward(received_grad, gate_act, up_act, w_gate, w_up, w_down):
    contract = (((1,), (1,)), ((), ()))
    grad_hidden = lax.dot_general(
        received_grad, w_down, contract, preferred_element_type=jnp.float32
    )
    sigma = jax.nn.sigmoid(gate_act)
    grad_gate = (grad_hidden * up_act * sigma * (1.0 + gate_act * (1.0 - sigma))).astype(
        jnp.bfloat16
    )
    grad_up = (grad_hidden * gate_act * sigma).astype(jnp.bfloat16)
    returned = lax.dot_general(grad_gate, w_gate, contract, preferred_element_type=jnp.float32)
    returned = returned + lax.dot_general(
        grad_up, w_up, contract, preferred_element_type=jnp.float32
    )
    return returned.astype(jnp.bfloat16)


def on_device(tokens, expert_ids, router_weight, gate_weight, up_weight, down_weight, grad_out):
    row_count, feature_dim = tokens.shape
    topk = expert_ids.shape[1]
    groups = lax.axis_size(("tp", "cp"))
    capacity = 3 * row_count * topk // (2 * groups)
    expert_count = router_weight.shape[1]
    contract = (((1,), (1,)), ((), ()))
    w_gate, w_up, w_down = (
        lax.all_gather(gate_weight[0], "dp", axis=0, tiled=True),
        lax.all_gather(up_weight[0], "dp", axis=0, tiled=True),
        lax.all_gather(down_weight[0], "dp", axis=1, tiled=True),
    )
    logits = jnp.dot(tokens, router_weight, preferred_element_type=jnp.float32)
    chosen = jnp.take_along_axis(logits, expert_ids, axis=1)
    mixing = 1.0 / jnp.sum(jnp.exp(chosen[:, None, :] - chosen[:, :, None]), axis=2)
    flat_ids = expert_ids.reshape(-1)
    slots = route_slots(flat_ids, expert_count)
    position = flat_ids * capacity + slots
    slot_total = groups * capacity
    repeated = jnp.repeat(tokens, topk, axis=0)
    scaled_grad = (mixing[:, :, None] * grad_out.astype(jnp.float32)[:, None, :]).astype(
        jnp.bfloat16
    )
    scaled_flat = scaled_grad.reshape(-1, feature_dim)
    sent = jnp.zeros((1, slot_total, feature_dim), jnp.bfloat16).at[0, position].set(repeated)
    received = trade(sent, capacity)[0]
    gate_act, up_act, produced = expert_forward(received, w_gate, w_up, w_down)
    came_back = trade(produced[None], capacity)[0]
    sent_grad = (
        jnp.zeros((1, slot_total, feature_dim), jnp.bfloat16).at[0, position].set(scaled_flat)
    )
    received_grad = trade(sent_grad, capacity)[0]
    returned = expert_backward(received_grad, gate_act, up_act, w_gate, w_up, w_down)
    back_home = trade(returned[None], capacity)[0]
    out_rows = jnp.take(came_back, position, axis=0).reshape(row_count, topk, feature_dim)
    moe_out = jnp.sum(mixing[:, :, None] * out_rows.astype(jnp.float32), axis=1).astype(
        jnp.bfloat16
    )
    back_rows = jnp.take(back_home, position, axis=0).reshape(row_count, topk, feature_dim)
    scores = jnp.einsum("td,tkd->tk", grad_out, out_rows, preferred_element_type=jnp.float32)
    dlogit = mixing * (scores - jnp.sum(mixing * scores, axis=1, keepdims=True))
    onehot = (
        expert_ids[:, :, None] == jnp.arange(expert_count, dtype=jnp.int32)[None, None, :]
    ).astype(jnp.float32)
    dense = jnp.sum(onehot * dlogit[:, :, None], axis=1).astype(jnp.bfloat16)
    router_back = lax.dot_general(
        dense, router_weight, contract, preferred_element_type=jnp.float32
    )
    grad_tokens = (jnp.sum(back_rows.astype(jnp.float32), axis=1) + router_back).astype(
        jnp.bfloat16
    )
    router_part = lax.dot_general(
        tokens, dense, (((0,), (0,)), ((), ())), preferred_element_type=jnp.float32
    )
    router_grad = lax.psum(router_part, ("dp", "tp", "cp"))
    return (moe_out, grad_tokens, router_grad)


def solution(mesh):
    in_specs = (
        P(("dp", "tp", "cp"), None),
        P(("dp", "tp", "cp"), None),
        P(),
        P(("tp", "cp"), "dp", None),
        P(("tp", "cp"), "dp", None),
        P(("tp", "cp"), None, "dp"),
        P(("dp", "tp", "cp"), None),
    )
    out_specs = (P(("dp", "tp", "cp"), None), P(("dp", "tp", "cp"), None), P())
    return jax.shard_map(
        on_device, mesh=mesh, in_specs=in_specs, out_specs=out_specs, check_vma=False
    )
```

profile of v0, /device:TPU:1, one launch (start us, length us, event | category | flops | bytes accessed | tf_op | source)
XLA Modules:
  0.0 453.8 jit_solution(12045069232960749352)
XLA Ops:
  7.2 0.7 broadcast_multiply_fusion
  7.9 0.8 copy.57
  9.2 0.6 reduce-window.6
  9.8 0.2 slice_reduce_fusion
  10.1 1.2 broadcast_in_dim.16
  11.3 0.2 reshape.137
  11.6 1.9 scatter_custom_fusion
  13.5 1.2 reshape.105
  14.7 10.6 %all-to-all-start = ((bf16[1,32,12,1024]{3,2,0,1:T(8,128)(2,1)}), bf16[1,32,12,1024]{3,2,0,1:T(8,128)(2,1)S(1)}, u32[]{:S(2)}, u32[]{:S(2)}) async-start(bf16[1,32,12,1024]{3,2,0,1:T(8,128)(2,1)} %bitcast.4), calls=%async_computation | async-start | bytes 2097152 | tf_op jit(solution)/shard_map/all_to_all | solution.py:21
  25.3 27.5 %all-gather.2 = bf16[1,384,1024]{1,2,0:T(8,128)(2,1)} all-gather(bf16[1,384,64]{1,2,0:T(8,128)(2,1)S(1)} %copy-done.15), channel_id=4, replica_groups=mesh['dp'=16,'tp'=4,'cp'=8] {'dp'}, dimensions={2}, use_global_device_ids=true | all-gather | bytes 835584 | tf_op jit(solution)/shard_map/all_gather | solution.py:60
  52.9 16.6 %all-gather.1 = bf16[1,1024,384]{2,1,0:T(8,128)(2,1)S(1)} all-gather(bf16[1,64,384]{2,1,0:T(8,128)(2,1)S(1)} %copy-done.16), channel_id=3, replica_groups=mesh['dp'=16,'tp'=4,'cp'=8] {'dp'}, dimensions={1}, use_global_device_ids=true | all-gather | bytes 835584 | tf_op jit(solution)/shard_map/all_gather | solution.py:59
  69.5 17.9 %all-gather = bf16[1,1024,384]{2,1,0:T(8,128)(2,1)S(1)} all-gather(bf16[1,64,384]{2,1,0:T(8,128)(2,1)S(1)} %copy-done.17), channel_id=2, replica_groups=mesh['dp'=16,'tp'=4,'cp'=8] {'dp'}, dimensions={1}, use_global_device_ids=true | all-gather | bytes 835584 | tf_op jit(solution)/shard_map/all_gather | solution.py:58
  87.4 0.2 squeeze_reshape.12
  87.6 0.6 fusion.5
  88.3 0.6 fusion.9
  88.9 0.2 copy-done.12
  89.1 0.8 copy-done.10
  89.9 0.6 convolution_convert_fusion
  90.5 1.2 reshape_broadcast_in_dim.6
  91.8 9.6 %all-to-all-start.1 = ((bf16[1,32,12,1024]{3,2,0,1:T(8,128)(2,1)}), bf16[1,32,12,1024]{3,2,0,1:T(8,128)(2,1)S(1)}, u32[]{:S(2)}, u32[]{:S(2)}) async-start(bf16[1,32,12,1024]{3,2,0,1:T(8,128)(2,1)} %bitcast.8), calls=%async_computation.1 | async-start | bytes 2097152 | tf_op jit(solution)/shard_map/all_to_all | solution.py:21
  101.9 2.0 gather_fusion
  104.1 0.3 mul.97
  104.4 1.7 mul.98
  106.1 21.9 %all-to-all-done.1 = bf16[1,32,12,1024]{3,2,0,1:T(8,128)(2,1)S(1)} async-done(((bf16[1,32,12,1024]{3,2,0,1:T(8,128)(2,1)}), bf16[1,32,12,1024]{3,2,0,1:T(8,128)(2,1)S(1)}, u32[]{:S(2)}, u32[]{:S(2)}) %all-to-all-start.1) | async-done | bytes 786464 | tf_op jit(solution)/shard_map/all_to_all | solution.py:21
  128.1 0.2 squeeze_reshape.13
  128.3 1.2 gather_fusion.1
  129.6 0.2 reshape.106
  129.8 1.1 fusion.13
  131.3 2.0 scatter_custom_fusion.1
  133.3 0.2 reshape.107
  133.5 33.6 %all_to_all.20 = bf16[1,32,12,1024]{3,2,0,1:T(8,128)(2,1)S(1)} all-to-all(bf16[1,32,12,1024]{3,2,0,1:T(8,128)(2,1)S(1)} %bitcast.72), channel_id=1, replica_groups=mesh['dp'=16,'tp'=4,'cp'=8] {'tp','cp'}, dimensions={1} | all-to-all | bytes 1572864 | tf_op jit(solution)/shard_map/all_to_all | solution.py:21
  167.1 0.2 squeeze_reshape.14
  167.3 1.8 fusion.1
  169.1 0.7 fusion.7
  169.9 0.4 copy-done.3
  170.3 0.6 add_convert_fusion
  170.9 1.2 reshape_broadcast_in_dim.7
  172.1 6.0 %all-to-all-start.3 = ((bf16[1,32,12,1024]{3,2,0,1:T(8,128)(2,1)}), bf16[1,32,12,1024]{3,2,0,1:T(8,128)(2,1)S(1)}, u32[]{:S(2)}, u32[]{:S(2)}) async-start(bf16[1,32,12,1024]{3,2,0,1:T(8,128)(2,1)} %bitcast.10), calls=%async_computation.3 | async-start | bytes 2097152 | tf_op jit(solution)/shard_map/all_to_all | solution.py:21
  178.2 0.8 convolution_bitcast_fusion
  179.0 2.1 multiply_reduce_fusion
  181.2 22.9 %all-to-all-done.3 = bf16[1,32,12,1024]{3,2,0,1:T(8,128)(2,1)S(1)} async-done(((bf16[1,32,12,1024]{3,2,0,1:T(8,128)(2,1)}), bf16[1,32,12,1024]{3,2,0,1:T(8,128)(2,1)S(1)}, u32[]{:S(2)}, u32[]{:S(2)}) %all-to-all-start.3) | async-done | bytes 786464 | tf_op jit(solution)/shard_map/all_to_all | solution.py:21
  204.0 0.2 squeeze_reshape.15
  204.2 1.2 gather_fusion.2
  205.5 0.6 reshape.108
  206.1 1.2 reduce_sum.60
  207.4 1.0 fusion
  208.3 237.0 %all-reduce.3.cloned.1.call-done = f32[1024,32]{0,1:T(8,128)} async-done(((f32[1024,32]{0,1:T(8,128)}), f32[1024,32]{0,1:T(8,128)}) %all-reduce.3.cloned.1.call-update) | async-done | bytes 131088 | tf_op jit(solution)/shard_map/psum | solution.py:104
  445.3 1.6 copy.73
  (65 shorter events, 2.2 us)
Async XLA Ops:
  7.2 94.5 %copy-start = (bf16[1024,32]{0,1:T(8,128)(2,1)S(1)}, bf16[1024,32]{0,1:T(8,128)(2,1)}, u32[]{:S(2)}) copy-start(bf16[1024,32]{0,1:T(8,128)(2,1)} %param.11) | copy-start | bytes 196612
  13.5 11.8 %copy-start.15 = (bf16[1,384,64]{1,2,0:T(8,128)(2,1)S(1)}, bf16[1,384,64]{1,2,0:T(8,128)(2,1)}, u32[]{:S(2)}) copy-start(bf16[1,384,64]{1,2,0:T(8,128)(2,1)} %param.14) | copy-start | bytes 147460
  14.7 38.2 %copy-start.16 = (bf16[1,64,384]{2,1,0:T(8,128)(2,1)S(1)}, bf16[1,64,384]{2,1,0:T(8,128)(2,1)}, u32[]{:S(2)}) copy-start(bf16[1,64,384]{2,1,0:T(8,128)(2,1)} %param.13) | copy-start | bytes 147460
  14.7 54.8 %copy-start.17 = (bf16[1,64,384]{2,1,0:T(8,128)(2,1)S(1)}, bf16[1,64,384]{2,1,0:T(8,128)(2,1)}, u32[]{:S(2)}) copy-start(bf16[1,64,384]{2,1,0:T(8,128)(2,1)} %param.12) | copy-start | bytes 147460
  14.7 72.7 %all-to-all-start = ((bf16[1,32,12,1024]{3,2,0,1:T(8,128)(2,1)}), bf16[1,32,12,1024]{3,2,0,1:T(8,128)(2,1)S(1)}, u32[]{:S(2)}, u32[]{:S(2)}) async-start(bf16[1,32,12,1024]{3,2,0,1:T(8,128)(2,1)} %bitcast.4), calls=%async_computation | async-start | bytes 2097152 | tf_op jit(solution)/shard_map/all_to_all | solution.py:21
  69.5 18.7 %copy-start.2 = (bf16[1,1024,384]{2,1,0:T(8,128)(2,1)}, bf16[1,1024,384]{2,1,0:T(8,128)(2,1)S(1)}, u32[]{:S(2)}) copy-start(bf16[1,1024,384]{2,1,0:T(8,128)(2,1)S(1)} %all-gather.1) | copy-start | bytes 2359300
  87.4 0.9 copy-start.4
  88.3 0.8 copy-start.12
  88.3 1.6 copy-start.6
  89.1 0.8 copy-start.10
  90.5 10.9 %copy-start.18 = (s32[128,2]{0,1:T(2,128)S(1)}, s32[128,2]{0,1:T(2,128)}, u32[]{:S(2)}) copy-start(s32[128,2]{0,1:T(2,128)} %param.10) | copy-start | bytes 3076
  91.8 9.9 %copy-start.7 = (bf16[128,1024]{1,0:T(8,128)(2,1)S(1)}, bf16[128,1024]{1,0:T(8,128)(2,1)}, u32[]{:S(2)}) copy-start(bf16[128,1024]{1,0:T(8,128)(2,1)} %param.9) | copy-start | bytes 786436
  91.8 36.3 %all-to-all-start.1 = ((bf16[1,32,12,1024]{3,2,0,1:T(8,128)(2,1)}), bf16[1,32,12,1024]{3,2,0,1:T(8,128)(2,1)S(1)}, u32[]{:S(2)}, u32[]{:S(2)}) async-start(bf16[1,32,12,1024]{3,2,0,1:T(8,128)(2,1)} %bitcast.8), calls=%async_computation.1 | async-start | bytes 2097152 | tf_op jit(solution)/shard_map/all_to_all | solution.py:21
  101.9 2.2 copy-start.14
  129.8 1.2 copy-start.8
  129.8 1.5 copy-start.1
  167.1 2.0 copy-start.5
  167.3 1.8 copy-start.11
  167.3 1.8 copy-start.13
  169.1 1.1 copy-start.3
  172.1 6.9 %copy-start.9 = (bf16[128,2,1024]{2,1,0:T(2,128)(2,1)S(1)}, bf16[128,2,1024]{2,1,0:T(2,128)(2,1)}, u32[]{:S(2)}) copy-start(bf16[128,2,1024]{2,1,0:T(2,128)(2,1)} %copy-done.8) | copy-start | bytes 1572868
  172.1 32.0 %all-to-all-start.3 = ((bf16[1,32,12,1024]{3,2,0,1:T(8,128)(2,1)}), bf16[1,32,12,1024]{3,2,0,1:T(8,128)(2,1)S(1)}, u32[]{:S(2)}, u32[]{:S(2)}) async-start(bf16[1,32,12,1024]{3,2,0,1:T(8,128)(2,1)} %bitcast.10), calls=%async_computation.3 | async-start | bytes 2097152 | tf_op jit(solution)/shard_map/all_to_all | solution.py:21
  178.1 267.3 %all-reduce.3.cloned.1.call-start = ((), (), s32[]{:S(2)}) async-start(), calls=%async_computation.4 | async-start | bytes 262144 | tf_op jit(solution)/shard_map/psum | solution.py:104
Sparse Core Ops, SparseCore 0:
  184.5 260.8 all-reduce.2
where the time goes:
time: 454 us
  waiting for transfers between devices  282 us (62%)
  blocking collectives  95.7 us (21%)
  starting transfers between devices  26.3 us (6%)
  local copies, waits for them, and re-layouts  20.4 us (4%)
  between operations  14.4 us (3%)
  matrix products  7.95 us (2%)
  other arithmetic  7.16 us (2%)
    psum x1, waiting for transfers between devices, on_device(): router_grad = lax.psum(router_part, ('dp', 'tp', 'cp'))  237 us
    all_to_all x3, waiting for transfers between devices, trade(): lax.all_to_all(shaped, ('tp', 'cp'), split_axis=1, concat_axis=1, tiled=T...  44.8 us
    all_to_all x1, blocking collectives, trade(): lax.all_to_all(shaped, ('tp', 'cp'), split_axis=1, concat_axis=1, tiled=T...  33.6 us
    all_gather x1, blocking collectives, on_device(): lax.all_gather(down_weight[0], 'dp', axis=1, tiled=True)  27.5 us
    all_to_all x3, starting transfers between devices, trade(): lax.all_to_all(shaped, ('tp', 'cp'), split_axis=1, concat_axis=1, tiled=T...  26.3 us
    all_gather x1, blocking collectives, on_device(): lax.all_gather(gate_weight[0], 'dp', axis=0, tiled=True)  17.9 us
    all_gather x1, blocking collectives, on_device(): lax.all_gather(up_weight[0], 'dp', axis=0, tiled=True)  16.6 us
  transfers between devices with their start and end apart: 4, of which 3 were waited for; matrix products, arithmetic and copies ran while one was open for 3% of the time, Pallas kernels for 0%

commit v1 on v0

--- a/solution.py
+++ b/solution.py
@@ -2,6 +2,24 @@
 import jax.numpy as jnp
 from jax import lax
 from jax.sharding import PartitionSpec as P
+
+
+def collect(array, axis, dim):
+    ways, here, turn = (lax.axis_size(axis), lax.axis_index(axis), array.shape[dim])
+    dims = [n * ways if d == dim else n for d, n in enumerate(array.shape)]
+    full = lax.dynamic_update_slice_in_dim(
+        jnp.zeros(dims, array.dtype), array, here * turn, axis=dim
+    )
+    going_up = going_down = array
+    for far in range(1, ways // 2 + 1):
+        going_up = lax.ppermute(going_up, axis, [(d, (d + 1) % ways) for d in range(ways)])
+        full = lax.dynamic_update_slice_in_dim(full, going_up, (here - far) % ways * turn, axis=dim)
+        if 2 * far < ways:
+            going_down = lax.ppermute(going_down, axis, [(d, (d - 1) % ways) for d in range(ways)])
+            full = lax.dynamic_update_slice_in_dim(
+                full, going_down, (here + far) % ways * turn, axis=dim
+            )
+    return full
 
 
 def route_slots(flat_ids, expert_count):
@@ -56,7 +74,7 @@
     contract = (((1,), (1,)), ((), ()))
     w_gate, w_up, w_down = (
         lax.all_gather(gate_weight[0], "dp", axis=0, tiled=True),
-        lax.all_gather(up_weight[0], "dp", axis=0, tiled=True),
+        collect(up_weight[0], "dp", 0),
         lax.all_gather(down_weight[0], "dp", axis=1, tiled=True),
     )
     logits = jnp.dot(tokens, router_weight, preferred_element_type=jnp.float32)

time: 454 us -> 468 us (1.031)
  blocking collectives: 95.7 us -> 72.4 us
  starting transfers between devices: 26.3 us -> 48.1 us
  local copies, waits for them, and re-layouts: 20.4 us -> 31.8 us
    ppermute x0 -> x15, starting transfers between devices: none -> 23.2 us  [the longest x7 13.1 us: collect(): lax.ppermute(going_down, axis, [(d, (d - 1) % ways) for d in range(ways)])]
    all_gather x1 -> x0, blocking collectives: 16.6 us -> none  [on_device(): lax.all_gather(up_weight[0], 'dp', axis=0, tiled=True)]
    dynamic_update_slice x0 -> x16, local copies, waits for them, and re-layouts: none -> 10.7 us  [the longest x8 5.79 us: collect(): lax.dynamic_update_slice_in_dim(full, going_up, (here - far) % ways * tur...]
  transfers between devices with their start and end apart: 4 -> 19, of which waited for: 3 -> 7; matrix products, arithmetic and copies ran while one was open for 3% -> 7% of each run, Pallas kernels for 0% -> 0%
where the time goes in v1:
time: 468 us
  waiting for transfers between devices  285 us (61%)
  blocking collectives  72.4 us (15%)
  starting transfers between devices  48.1 us (10%)
  local copies, waits for them, and re-layouts  31.8 us (7%)
  between operations  14.5 us (3%)
  matrix products  9 us (2%)
  other arithmetic  7.13 us (2%)
    psum x1, waiting for transfers between devices, on_device(): router_grad = lax.psum(router_part, ('dp', 'tp', 'cp'))  240 us
    all_to_all x3, waiting for transfers between devices, trade(): lax.all_to_all(shaped, ('tp', 'cp'), split_axis=1, concat_axis=1, tiled=T...  40.8 us
    all_to_all x1, blocking collectives, trade(): lax.all_to_all(shaped, ('tp', 'cp'), split_axis=1, concat_axis=1, tiled=T...  30.5 us
    all_gather x1, blocking collectives, on_device(): lax.all_gather(down_weight[0], 'dp', axis=1, tiled=True)  25.2 us
    all_to_all x3, starting transfers between devices, trade(): lax.all_to_all(shaped, ('tp', 'cp'), split_axis=1, concat_axis=1, tiled=T...  24.7 us
    all_gather x1, blocking collectives, on_device(): lax.all_gather(gate_weight[0], 'dp', axis=0, tiled=True)  16.6 us
    ppermute x7, starting transfers between devices, collect(): lax.ppermute(going_down, axis, [(d, (d - 1) % ways) for d in range(ways)])  13.1 us
    ppermute x8, starting transfers between devices, collect(): lax.ppermute(going_up, axis, [(d, (d + 1) % ways) for d in range(ways)])  10 us
  transfers between devices with their start and end apart: 19, of which 7 were waited for; matrix products, arithmetic and copies ran while one was open for 7% of the time, Pallas kernels for 0%

profile of v1, /device:TPU:1, one launch (start us, length us, event | category | flops | bytes accessed | tf_op | source)
XLA Modules:
  0.0 467.5 jit_solution(3872345055317075802)
XLA Ops:
  7.2 3.5 collective-permute-start
  10.7 3.4 collective-permute-start.1
  14.1 0.7 broadcast_multiply_fusion
  14.8 0.8 copy.57
  16.9 1.2 broadcast_in_dim.18
  18.5 1.9 scatter_custom_fusion
  20.4 1.1 reshape.105
  21.6 6.4 %all-to-all-start = ((bf16[1,32,12,1024]{3,2,0,1:T(8,128)(2,1)}), bf16[1,32,12,1024]{3,2,0,1:T(8,128)(2,1)S(1)}, u32[]{:S(2)}, u32[]{:S(2)}) async-start(bf16[1,32,12,1024]{3,2,0,1:T(8,128)(2,1)} %bitcast.4), calls=%async_computation | async-start | bytes 2097152 | tf_op jit(solution)/shard_map/all_to_all | solution.py:39
  28.0 25.2 %all-gather.1 = bf16[1,384,1024]{1,2,0:T(8,128)(2,1)S(1)} all-gather(bf16[1,384,64]{1,2,0:T(8,128)(2,1)S(1)} %copy-done.14), channel_id=3, replica_groups=mesh['dp'=16,'tp'=4,'cp'=8] {'dp'}, dimensions={2}, use_global_device_ids=true | all-gather | bytes 835584 | tf_op jit(solution)/shard_map/all_gather | solution.py:78
  53.2 16.6 %all-gather = bf16[1,1024,384]{2,1,0:T(8,128)(2,1)S(1)} all-gather(bf16[1,64,384]{2,1,0:T(8,128)(2,1)S(1)} %copy-done.15), channel_id=2, replica_groups=mesh['dp'=16,'tp'=4,'cp'=8] {'dp'}, dimensions={1}, use_global_device_ids=true | all-gather | bytes 835584 | tf_op jit(solution)/shard_map/all_gather | solution.py:76
  69.8 1.0 broadcast_in_dim.19
  71.4 1.4 collective-permute-start.2
  72.9 1.4 constant_dynamic-update-slice_fusion.13
  74.9 1.7 collective-permute-start.4
  76.7 0.6 constant_dynamic-update-slice_fusion.11
  77.9 2.3 collective-permute-start.6
  80.5 0.9 collective-permute-start.7
  82.6 1.1 collective-permute-start.8
  84.0 2.1 collective-permute-start.9
  86.1 0.6 constant_dynamic-update-slice_fusion.7
  86.7 0.6 constant_dynamic-update-slice_fusion.6
  87.5 3.3 collective-permute-start.11
  92.0 3.5 collective-permute-start.13
  96.1 0.6 constant_dynamic-update-slice_fusion.2
  96.8 0.6 constant_dynamic-update-slice_fusion.1
  98.0 2.9 collective-permute-done.14
  101.8 1.7 fusion.30
  105.2 1.2 reshape_broadcast_in_dim.6
  106.4 9.8 %all-to-all-start.1 = ((bf16[1,32,12,1024]{3,2,0,1:T(8,128)(2,1)}), bf16[1,32,12,1024]{3,2,0,1:T(8,128)(2,1)S(1)}, u32[]{:S(2)}, u32[]{:S(2)}) async-start(bf16[1,32,12,1024]{3,2,0,1:T(8,128)(2,1)} %bitcast.8), calls=%async_computation.1 | async-start | bytes 2097152 | tf_op jit(solution)/shard_map/all_to_all | solution.py:39
  116.6 2.0 gather_fusion
  119.2 1.7 mul.162
  120.9 18.6 %all-to-all-done.1 = bf16[1,32,12,1024]{3,2,0,1:T(8,128)(2,1)S(1)} async-done(((bf16[1,32,12,1024]{3,2,0,1:T(8,128)(2,1)}), bf16[1,32,12,1024]{3,2,0,1:T(8,128)(2,1)S(1)}, u32[]{:S(2)}, u32[]{:S(2)}) %all-to-all-start.1) | async-done | bytes 786464 | tf_op jit(solution)/shard_map/all_to_all | solution.py:39
  139.7 1.2 gather_fusion.1
  141.2 1.1 fusion.10
  142.7 2.0 scatter_custom_fusion.1
  144.9 30.5 %all_to_all.20 = bf16[1,32,12,1024]{3,2,0,1:T(8,128)(2,1)S(1)} all-to-all(bf16[1,32,12,1024]{3,2,0,1:T(8,128)(2,1)S(1)} %bitcast.71), channel_id=1, replica_groups=mesh['dp'=16,'tp'=4,'cp'=8] {'tp','cp'}, dimensions={1} | all-to-all | bytes 1572864 | tf_op jit(solution)/shard_map/all_to_all | solution.py:39
  177.1 0.7 fusion.4
  177.8 1.8 add_convert_fusion
  179.6 1.1 reshape_broadcast_in_dim.7
  180.7 8.5 %all-to-all-start.3 = ((bf16[1,32,12,1024]{3,2,0,1:T(8,128)(2,1)}), bf16[1,32,12,1024]{3,2,0,1:T(8,128)(2,1)S(1)}, u32[]{:S(2)}, u32[]{:S(2)}) async-start(bf16[1,32,12,1024]{3,2,0,1:T(8,128)(2,1)} %bitcast.10), calls=%async_computation.3 | async-start | bytes 2097152 | tf_op jit(solution)/shard_map/all_to_all | solution.py:39
  189.5 0.8 convolution_bitcast_fusion
  190.4 2.1 multiply_reduce_fusion
  192.5 22.2 %all-to-all-done.3 = bf16[1,32,12,1024]{3,2,0,1:T(8,128)(2,1)S(1)} async-done(((bf16[1,32,12,1024]{3,2,0,1:T(8,128)(2,1)}), bf16[1,32,12,1024]{3,2,0,1:T(8,128)(2,1)S(1)}, u32[]{:S(2)}, u32[]{:S(2)}) %all-to-all-start.3) | async-done | bytes 786464 | tf_op jit(solution)/shard_map/all_to_all | solution.py:39
  214.9 1.2 gather_fusion.2
  216.8 1.2 reduce_sum.60
  218.1 1.0 fusion
  219.0 240.1 %all-reduce.3.cloned.1.call-done = f32[1024,32]{0,1:T(8,128)} async-done(((f32[1024,32]{0,1:T(8,128)}), f32[1024,32]{0,1:T(8,128)}) %all-reduce.3.cloned.1.call-update) | async-done | bytes 131088 | tf_op jit(solution)/shard_map/psum | solution.py:122
  459.1 1.6 copy.89
  (109 shorter events, 15.4 us)
Async XLA Ops:
  7.2 109.3 %copy-start = (bf16[1024,32]{0,1:T(8,128)(2,1)S(1)}, bf16[1024,32]{0,1:T(8,128)(2,1)}, u32[]{:S(2)}) copy-start(bf16[1024,32]{0,1:T(8,128)(2,1)} %param.11) | copy-start | bytes 196612
  7.2 64.3 %collective-permute-start = (bf16[64,384]{1,0:T(8,128)(2,1)}, bf16[64,384]{1,0:T(8,128)(2,1)}, u32[]{:S(2)}, u32[]{:S(2)}) collective-permute-start(bf16[64,384]{1,0:T(8,128)(2,1)} %bitcast.73), channel_id=1, source_target_pairs={{0,32},{32,64},{64,96},{96,128},{128,160},{160,192},{192,224},{224... | collective-permute-start | bytes 147464 | tf_op jit(solution)/shard_map/ppermute | solution.py:15
  10.7 62.2 %collective-permute-start.1 = (bf16[64,384]{1,0:T(8,128)(2,1)}, bf16[64,384]{1,0:T(8,128)(2,1)S(1)}, u32[]{:S(2)}, u32[]{:S(2)}) collective-permute-start(bf16[64,384]{1,0:T(8,128)(2,1)} %bitcast.74), channel_id=1, source_target_pairs={{0,480},{32,0},{64,32},{96,64},{128,96},{160,128},{192,160},{224,1... | collective-permute-start | bytes 147464 | tf_op jit(solution)/shard_map/ppermute | solution.py:18
  20.4 7.6 %copy-start.14 = (bf16[1,384,64]{1,2,0:T(8,128)(2,1)S(1)}, bf16[1,384,64]{1,2,0:T(8,128)(2,1)}, u32[]{:S(2)}) copy-start(bf16[1,384,64]{1,2,0:T(8,128)(2,1)} %param.14) | copy-start | bytes 147460
  21.6 31.6 %copy-start.15 = (bf16[1,64,384]{2,1,0:T(8,128)(2,1)S(1)}, bf16[1,64,384]{2,1,0:T(8,128)(2,1)}, u32[]{:S(2)}) copy-start(bf16[1,64,384]{2,1,0:T(8,128)(2,1)} %param.12) | copy-start | bytes 147460
  21.6 80.0 %all-to-all-start = ((bf16[1,32,12,1024]{3,2,0,1:T(8,128)(2,1)}), bf16[1,32,12,1024]{3,2,0,1:T(8,128)(2,1)S(1)}, u32[]{:S(2)}, u32[]{:S(2)}) async-start(bf16[1,32,12,1024]{3,2,0,1:T(8,128)(2,1)} %bitcast.4), calls=%async_computation | async-start | bytes 2097152 | tf_op jit(solution)/shard_map/all_to_all | solution.py:39
  28.0 42.9 %copy-start.16 = (bf16[1,64,384]{2,1,0:T(8,128)(2,1)S(1)}, bf16[1,64,384]{2,1,0:T(8,128)(2,1)}, u32[]{:S(2)}) copy-start(bf16[1,64,384]{2,1,0:T(8,128)(2,1)} %param.13) | copy-start | bytes 147460
  53.2 50.9 %copy-start.2 = (bf16[1,384,1024]{1,2,0:T(8,128)(2,1)}, bf16[1,384,1024]{1,2,0:T(8,128)(2,1)S(1)}, u32[]{:S(2)}) copy-start(bf16[1,384,1024]{1,2,0:T(8,128)(2,1)S(1)} %all-gather.1) | copy-start | bytes 2359300
  69.8 33.7 %copy-start.4 = (bf16[1,1024,384]{2,1,0:T(8,128)(2,1)}, bf16[1,1024,384]{2,1,0:T(8,128)(2,1)S(1)}, u32[]{:S(2)}) copy-start(bf16[1,1024,384]{2,1,0:T(8,128)(2,1)S(1)} %all-gather) | copy-start | bytes 2359300
  71.4 3.5 collective-permute-start.2
  72.9 3.8 collective-permute-start.3
  74.9 3.0 collective-permute-start.4
  76.7 3.8 collective-permute-start.5
  77.9 4.7 collective-permute-start.6
  80.5 3.5 collective-permute-start.7
  82.6 4.7 %collective-permute-start.8 = (bf16[64,384]{1,0:T(8,128)(2,1)S(1)}, bf16[64,384]{1,0:T(8,128)(2,1)S(1)}, u32[]{:S(2)}, u32[]{:S(2)}) collective-permute-start(bf16[64,384]{1,0:T(8,128)(2,1)S(1)} %collective-permute-done.6), channel_id=1, source_target_pairs={{0,32},{32,64},{64,96},{96,128},{128,160},{160,192},{192,224},{224... | collective-permute-start | bytes 147464 | tf_op jit(solution)/shard_map/ppermute | solution.py:15
  84.0 3.5 collective-permute-start.9
  87.3 4.7 %collective-permute-start.10 = (bf16[64,384]{1,0:T(8,128)(2,1)S(1)}, bf16[64,384]{1,0:T(8,128)(2,1)S(1)}, u32[]{:S(2)}, u32[]{:S(2)}) collective-permute-start(bf16[64,384]{1,0:T(8,128)(2,1)S(1)} %collective-permute-done.8), channel_id=1, source_target_pairs={{0,32},{32,64},{64,96},{96,128},{128,160},{160,192},{192,224},{224... | collective-permute-start | bytes 147464 | tf_op jit(solution)/shard_map/ppermute | solution.py:15
  87.5 4.5 collective-permute-start.11
  92.0 4.8 %collective-permute-start.12 = (bf16[64,384]{1,0:T(8,128)(2,1)S(1)}, bf16[64,384]{1,0:T(8,128)(2,1)S(1)}, u32[]{:S(2)}, u32[]{:S(2)}) collective-permute-start(bf16[64,384]{1,0:T(8,128)(2,1)S(1)} %collective-permute-done.10), channel_id=1, source_target_pairs={{0,32},{32,64},{64,96},{96,128},{128,160},{160,192},{192,224},{224... | collective-permute-start | bytes 147464 | tf_op jit(solution)/shard_map/ppermute | solution.py:15
  92.0 5.4 %collective-permute-start.13 = (bf16[64,384]{1,0:T(8,128)(2,1)S(1)}, bf16[64,384]{1,0:T(8,128)(2,1)S(1)}, u32[]{:S(2)}, u32[]{:S(2)}) collective-permute-start(bf16[64,384]{1,0:T(8,128)(2,1)S(1)} %collective-permute-done.11), channel_id=1, source_target_pairs={{0,480},{32,0},{64,32},{96,64},{128,96},{160,128},{192,160},{224,1... | collective-permute-start | bytes 147464 | tf_op jit(solution)/shard_map/ppermute | solution.py:18
  96.8 4.2 collective-permute-start.14
  103.5 0.8 copy-start.11
  104.3 0.8 copy-start.9
  105.2 11.0 %copy-start.17 = (s32[128,2]{0,1:T(2,128)S(1)}, s32[128,2]{0,1:T(2,128)}, u32[]{:S(2)}) copy-start(s32[128,2]{0,1:T(2,128)} %param.10) | copy-start | bytes 3076
  106.4 10.1 %copy-start.6 = (bf16[128,1024]{1,0:T(8,128)(2,1)S(1)}, bf16[128,1024]{1,0:T(8,128)(2,1)}, u32[]{:S(2)}) copy-start(bf16[128,1024]{1,0:T(8,128)(2,1)} %param.9) | copy-start | bytes 786436
  106.4 33.1 %all-to-all-start.1 = ((bf16[1,32,12,1024]{3,2,0,1:T(8,128)(2,1)}), bf16[1,32,12,1024]{3,2,0,1:T(8,128)(2,1)S(1)}, u32[]{:S(2)}, u32[]{:S(2)}) async-start(bf16[1,32,12,1024]{3,2,0,1:T(8,128)(2,1)} %bitcast.8), calls=%async_computation.1 | async-start | bytes 2097152 | tf_op jit(solution)/shard_map/all_to_all | solution.py:39
  116.6 2.2 copy-start.13
  141.2 1.2 copy-start.7
  141.2 1.5 copy-start.1
  144.9 30.7 %copy-start.3 = (bf16[1,384,1024]{1,2,0:T(8,128)(2,1)S(1)}, bf16[1,384,1024]{1,2,0:T(8,128)(2,1)}, u32[]{:S(2)}) copy-start(bf16[1,384,1024]{1,2,0:T(8,128)(2,1)} %copy-done.2) | copy-start | bytes 2359300
  175.6 1.1 copy-start.5
  175.6 1.3 copy-start.10
  175.6 1.5 copy-start.12
  180.7 9.7 %copy-start.8 = (bf16[128,2,1024]{2,1,0:T(2,128)(2,1)S(1)}, bf16[128,2,1024]{2,1,0:T(2,128)(2,1)}, u32[]{:S(2)}) copy-start(bf16[128,2,1024]{2,1,0:T(2,128)(2,1)} %copy-done.7) | copy-start | bytes 1572868
  180.7 34.0 %all-to-all-start.3 = ((bf16[1,32,12,1024]{3,2,0,1:T(8,128)(2,1)}), bf16[1,32,12,1024]{3,2,0,1:T(8,128)(2,1)S(1)}, u32[]{:S(2)}, u32[]{:S(2)}) async-start(bf16[1,32,12,1024]{3,2,0,1:T(8,128)(2,1)} %bitcast.10), calls=%async_computation.3 | async-start | bytes 2097152 | tf_op jit(solution)/shard_map/all_to_all | solution.py:39
  189.2 269.9 %all-reduce.3.cloned.1.call-start = ((), (), s32[]{:S(2)}) async-start(), calls=%async_computation.4 | async-start | bytes 262144 | tf_op jit(solution)/shard_map/psum | solution.py:122
Sparse Core Ops, SparseCore 0:
  195.6 263.4 all-reduce.2
